TPU v7x, 32 devices: a whole 2x2x4 slice. The times are simulated.
32 devices in a mesh: sta: 8 (over z, y), seg: 4 (over x, core).
Axes of the slice: x: 2, y: 2, z: 4, core: 2. Of those that a mesh axis runs over, the one named last changes fastest.
Arguments:
- spectra: bfloat16 [48, 16, 2, 1024], P('sta', 'seg'), may hold values from -6 to 6
- observed: float32 [40, 6, 6, 512], P('sta'), may hold values from -8 to 8
- pair_table: int32 [40, 2], P('sta'), may hold values from -1 to 7, as said below
Outputs:
- gradient: float32 [48, 2, 1024], P('sta', None, 'seg')
Inputs may be any that keep to these rules, and one draw needn't show every extreme that they name: `pair_table`: rows are slots; each unordered pair of station blocks p <= q of the 8 blocks stands in exactly one row as (p, q); every other row is (-1, -1).
All inputs are finite; a program needn't handle non-finite values.
Results may differ from a plain program's by a relative error of at most 0.0013.
Values may be sent and summed in bfloat16 or wider, within the bound.
No kernel may reach another device: no remote copies, remote signals or barrier semaphores. Data moves between devices by JAX's collectives and lax.ppermute only.
A program may use at most 64 MiB of HBM per device.

v0:
```python
import math
import jax
import jax.numpy as jnp
from jax import lax
from jax.sharding import PartitionSpec as P

F = 1024
LAGS = 512


def lag_kernel(start, count):
    frequency = (start + jnp.arange(count, dtype=jnp.int32))[:, None]
    offset = jnp.arange(LAGS, dtype=jnp.int32)[None, :] - LAGS // 2
    phase = jnp.mod(frequency * offset, 2 * F)
    angle = math.pi / F * phase.astype(jnp.float32)
    return jnp.stack([jnp.cos(angle), -jnp.sin(angle)], axis=0).astype(jnp.bfloat16)


def group_cross(left, right, groups):
    station_count = left.shape[0]
    left = left.reshape(station_count, groups, -1, 2, left.shape[-1]).astype(jnp.float32)
    right = right.reshape(station_count, groups, -1, 2, right.shape[-1]).astype(jnp.float32)
    left_real = left[:, :, :, 0][:, None]
    left_imag = left[:, :, :, 1][:, None]
    right_real = right[:, :, :, 0][None]
    right_imag = right[:, :, :, 1][None]
    cross_real = jnp.sum(left_real * right_real + left_imag * right_imag, axis=3)
    cross_imag = jnp.sum(left_imag * right_real - left_real * right_imag, axis=3)
    return jnp.stack([cross_real, cross_imag], axis=3).astype(jnp.bfloat16)


def slot_cross(gathered, starts_all, station_count, groups):

    def one_slot(starts):
        left = lax.dynamic_slice_in_dim(gathered, starts[0], station_count, 0)
        right = lax.dynamic_slice_in_dim(gathered, starts[1], station_count, 0)
        return group_cross(left, right, groups)

    return lax.map(one_slot, starts_all)


def pair_mask(first, second, station_count):
    row_index = jnp.arange(station_count)[:, None]
    col_index = jnp.arange(station_count)[None, :]
    keep = (first >= 0)[..., None, None] & (
        (first != second)[..., None, None] | (row_index < col_index)
    )
    return keep.astype(jnp.float32)


def adjoint_terms(gamma, stacked):
    gamma_real = gamma[..., 0, :]
    gamma_imag = gamma[..., 1, :]
    stack_real = stacked[..., 0, :]
    stack_imag = stacked[..., 1, :]
    common = gamma_real * stack_real + gamma_imag * stack_imag
    twist = gamma_imag * stack_real - gamma_real * stack_imag
    left_term = jnp.stack([common.sum(-2), twist.sum(-2)], axis=-2)
    right_term = jnp.stack([common.sum(-3), -twist.sum(-3)], axis=-2)
    return (left_term, right_term)


def on_device(spectra, observed, pair_table):
    station_dev = spectra.shape[0]
    slot_count = pair_table.shape[0]
    seg_devices = lax.axis_size("seg")
    scale = 1.0 / math.sqrt(F * spectra.shape[1] * seg_devices)
    first = pair_table[:, 0]
    second = pair_table[:, 1]
    starts_all = jnp.maximum(pair_table, 0) * station_dev
    keep = pair_mask(first, second, station_dev).reshape(-1, 1)
    observe_flat = observed.reshape(-1, LAGS)
    local = lax.all_to_all(spectra, "seg", split_axis=3, concat_axis=1, tiled=True)
    gathered = lax.all_gather(local, "sta", axis=0, tiled=True)
    width = local.shape[3]
    crossed = slot_cross(gathered, starts_all, station_dev, seg_devices)
    stacked = jnp.sum(lax.optimization_barrier(crossed).astype(jnp.float32), axis=3)
    kernel = lag_kernel(lax.axis_index("seg") * width, width)
    exact = lax.optimization_barrier(kernel).astype(jnp.float32)
    lag_terms = jnp.dot(
        stacked.reshape(-1, 2 * width),
        exact.reshape(2 * width, LAGS),
        precision=lax.Precision.HIGHEST,
    )
    lag_sum = lax.psum(lag_terms, "seg")
    residual = (keep * jnp.tanh(scale * lag_sum - observe_flat)).astype(jnp.bfloat16)
    matrix = kernel.reshape(2 * width, LAGS)
    gamma = scale * lax.dot_general(
        residual, matrix, (((1,), (1,)), ((), ())), preferred_element_type=jnp.float32
    )
    gamma = gamma.reshape(slot_count, station_dev, station_dev, 2, width)
    left_term, right_term = adjoint_terms(gamma, stacked)
    blocks = lax.axis_size("sta")
    block_index = jnp.arange(blocks)[None, :]
    choose_left = (first[:, None] == block_index).astype(jnp.float32)
    choose_right = (second[:, None] == block_index).astype(jnp.float32)
    contract = (((0,), (0,)), ((), ()))
    buffer = lax.dot_general(
        choose_left, left_term.reshape(slot_count, -1), contract, precision=lax.Precision.HIGHEST
    )
    buffer = buffer + lax.dot_general(
        choose_right, right_term.reshape(slot_count, -1), contract, precision=lax.Precision.HIGHEST
    )
    buffer = buffer.reshape(blocks * station_dev, 2, width)
    result = lax.psum_scatter(buffer, "sta", scatter_dimension=0, tiled=True)
    return result


def solution(mesh):
    placed = (P("sta", "seg", None, None), P("sta", None, None, None), P("sta", None))
    return jax.shard_map(
        on_device, mesh=mesh, in_specs=placed, out_specs=P("sta", None, "seg"), check_vma=False
    )
```

profile of v0, /device:TPU:0, one launch (start us, length us, event | category | flops | bytes accessed | tf_op | source)
XLA Modules:
  0.0 208.0 jit_solution(6341141259934463326)
XLA Ops:
  6.5 2.7 %copy.23 = bf16[6,4,2,1024]{0,1,2,3:T(4,128)(2,1)S(1)} copy(bf16[6,4,2,1024]{3,2,1,0:T(2,128)(2,1)} %param.5) | data formatting | bytes 196608 | tf_op args[0]
  9.2 4.1 %reshape.288 = bf16[4,2,6144]{2,1,0:T(2,128)(2,1)} reshape(bf16[1024,2,4,6]{3,2,1,0:T(4,128)(2,1)S(1)} %bitcast.64) | data formatting | bytes 196608
  13.3 4.2 %all-to-all-start = ((bf16[4,2,6144]{2,1,0:T(2,128)(2,1)}), bf16[4,2,6144]{2,1,0:T(2,128)(2,1)S(1)}, u32[]{:S(2)}, u32[]{:S(2)}) async-start(bf16[4,2,6144]{2,1,0:T(2,128)(2,1)} %reshape.288), calls=%async_computation | async-start | bytes 196608 | tf_op jit(solution)/shard_map/all_to_all | solution.py:73
  17.6 2.5 %fusion.3 = (bf16[1,256,512]{2,1,0:T(8,128)(2,1)S(1)}, bf16[1,256,512]{2,1,0:T(8,128)(2,1)S(1)}) fusion(s32[512]{0:T(512)S(1)} %iota_add_fusion, s32[256]{0:T(256)S(1)} %iota_add_fusion.1), kind=kLoop, calls=%fused_computation.26 | loop fusion | flops 2228224 | bytes 527360 | tf_op jit(solution)/shard_map/cos | solution.py:16
  20.1 0.1 and_convert_fusion
  20.2 0.1 maximum_convert_fusion
  20.2 0.1 reshape.286
  20.4 0.1 reshape.279
  20.4 1.4 all-to-all-done
  21.9 4.8 %reshape.289 = bf16[1024,2,4,6]{3,2,1,0:T(4,128)(2,1)S(1)} reshape(bf16[4,2,6144]{2,1,0:T(2,128)(2,1)S(1)} %all-to-all-done) | data formatting | bytes 196608
  26.6 1.8 copy.24
  28.4 33.1 %all_gather.3 = bf16[48,16,2,256]{3,1,2,0:T(8,128)(2,1)S(1)} all-gather(bf16[6,16,2,256]{3,1,2,0:T(8,128)(2,1)S(1)} %all_to_all.16), channel_id=1, replica_groups=mesh['sta'=8,'seg'=4] {'sta'}, dimensions={0}, use_global_device_ids=true | all-gather | bytes 884736 | tf_op jit(solution)/shard_map/all_gather | solution.py:74
  61.5 0.1 copy.25
  61.6 28.5 %while.10 = (s32[]{:T(128)}, bf16[5,6,6,4,2,256]{5,3,2,1,4,0:T(4,128)(2,1)S(1)}, s32[5,2]{0,1:T(2,128)S(1)}, bf16[48,16,2,256]{3,1,0,2:T(8,128)(2,1)S(1)}, s32[]{:T(128)}, /*index=5*/s32[]{:T(128)}, s32[]{:T(128)}) while((s32[]{:T(128)}, bf16[5,6,6,4,2,256]{5,3,2,1,4,0:T(4,128)(2,1)S(1)}, s32[5,2]{0,1:T(2,128)S(1)}, ...), condition=%wide.region_3.4_spmd, body=%wide.region_0.3_spmd.sunk | while | flops 1499144 | bytes 2998465 | solution.py:39
  61.6 0.1 constant_dynamic-slice_fusion.3
  61.7 0.6 fusion.24
  66.1 0.1 reshape.292
  66.1 0.1 reshape.293
  66.2 0.9 add_reduce_fusion.2
  67.2 0.1 maximum_dynamic-update-slice_fusion.2
  67.3 0.1 constant_dynamic-slice_fusion.3
  67.3 0.6 fusion.24
  71.7 0.1 reshape.292
  71.8 0.1 reshape.293
  71.9 0.9 add_reduce_fusion.2
  72.9 0.1 maximum_dynamic-update-slice_fusion.2
  73.0 0.1 constant_dynamic-slice_fusion.3
  73.0 0.6 fusion.24
  77.4 0.1 reshape.292
  77.5 0.1 reshape.293
  77.6 0.9 add_reduce_fusion.2
  78.6 0.1 maximum_dynamic-update-slice_fusion.2
  78.7 0.1 constant_dynamic-slice_fusion.3
  78.7 0.6 fusion.24
  83.1 0.1 reshape.292
  83.2 0.1 reshape.293
  83.3 0.9 add_reduce_fusion.2
  84.2 0.1 maximum_dynamic-update-slice_fusion.2
  84.4 0.1 constant_dynamic-slice_fusion.3
  84.4 0.6 fusion.24
  88.8 0.1 reshape.292
  88.9 0.1 reshape.293
  89.0 0.9 add_reduce_fusion.2
  89.9 0.1 maximum_dynamic-update-slice_fusion.2
  90.0 0.9 convert_reduce_fusion
  91.0 0.3 copy.26
  91.3 0.1 pad.8
  91.5 1.2 fusion.17
  92.8 32.7 %all-reduce.4.cloned.1.call-done = f32[180,512]{1,0:T(8,128)} async-done(((f32[180,512]{1,0:T(8,128)}), f32[180,512]{1,0:T(8,128)}) %all-reduce.4.cloned.1.call-update) | async-done | bytes 368656 | tf_op jit(solution)/shard_map/psum | solution.py:85
  125.4 1.3 convolution_multiply_fusion
  126.8 0.2 reshape.280
  127.0 0.3 fusion.16
  127.3 0.1 fusion.4
  127.4 0.2 fusion.13
  127.6 0.1 pad_maximum_fusion
  127.7 0.1 reshape.281
  127.8 0.1 pad_maximum_fusion.1
  127.9 0.1 reshape.282
  128.0 0.3 fusion.8
  128.3 0.3 convolution_add_fusion
  128.6 0.7 reshape.283
  129.3 0.6 dynamic-slice
  130.6 69.3 %all-reduce.6.cloned.1.call-done = f32[48,2,256]{2,1,0:T(2,128)} async-done(((f32[48,2,256]{2,1,0:T(2,128)}), f32[48,2,256]{2,1,0:T(2,128)}) %all-reduce.6.cloned.1.call-update) | async-done | bytes 98320
  199.9 1.3 constant_dynamic-slice_fusion.1
  (36 shorter events, 0.6 us)
Async XLA Ops:
  6.5 11.0 %copy-start.2 = (s32[5,2]{0,1:T(2,128)S(1)}, s32[5,2]{0,1:T(2,128)}, u32[]{:S(2)}) copy-start(s32[5,2]{0,1:T(2,128)} %param.7) | copy-start | bytes 124
  9.2 11.1 %copy-start.1 = (f32[5,6,6,512]{3,2,1,0:T(8,128)S(1)}, f32[5,6,6,512]{3,2,1,0:T(8,128)}, u32[]{:S(2)}) copy-start(f32[5,6,6,512]{3,2,1,0:T(8,128)} %param.6) | copy-start | bytes 1105924
  13.3 8.5 %all-to-all-start = ((bf16[4,2,6144]{2,1,0:T(2,128)(2,1)}), bf16[4,2,6144]{2,1,0:T(2,128)(2,1)S(1)}, u32[]{:S(2)}, u32[]{:S(2)}) async-start(bf16[4,2,6144]{2,1,0:T(2,128)(2,1)} %reshape.288), calls=%async_computation | async-start | bytes 196608 | tf_op jit(solution)/shard_map/all_to_all | solution.py:73
  17.6 107.9 %all-reduce.4.cloned.1.call-start = ((), (), s32[]{:S(2)}) async-start(), calls=%async_computation.1 | async-start | bytes 753664 | tf_op jit(solution)/shard_map/psum | solution.py:85
  28.4 33.2 %copy-start = (bf16[5,6,6,4,2,256]{5,3,2,1,4,0:T(4,128)(2,1)S(1)}, bf16[5,6,6,4,2,256]{5,3,2,1,4,0:T(4,128)(2,1)}, u32[]{:S(2)}) copy-start(bf16[5,6,6,4,2,256]{5,3,2,1,4,0:T(4,128)(2,1)} %custom-call) | copy-start | bytes 2211844
  92.7 107.2 %all-reduce.6.cloned.1.call-start = ((), (), s32[]{:S(2)}) async-start(), calls=%async_computation.2 | async-start | bytes 196608
  127.0 2.3 %copy-start.3 = (u32[32]{0:T(128)S(1)}, u32[32]{0:T(128)}, u32[]{:S(2)}) copy-start(u32[32]{0:T(128)} %constant.56) | copy-start | bytes 388
Sparse Core Ops, SparseCore 0:
  92.8 32.5 all-reduce.3
  129.4 70.4 all-reduce.5
where the time goes:
time: 209 us; the launch traced here: 208 us
  waiting for transfers between devices  103 us (49%)
  blocking collectives  33.1 us (16%)
  local copies, waits for them, and re-layouts  21.4 us (10%)
  loops' own time  19 us (9%)
  between operations  14.4 us (7%)
  other arithmetic  9.29 us (4%)
  starting transfers between devices  4.28 us (2%)
  matrix products  3.13 us (1%)
    unnamed x3, waiting for transfers between devices  69.4 us
    all_gather x1, blocking collectives, on_device(): gathered = lax.all_gather(local, 'sta', axis=0, tiled=True)  33.1 us
    psum x1, waiting for transfers between devices, on_device(): lag_sum = lax.psum(lag_terms, 'seg')  32.7 us
    another operation x1, loops' own time, slot_cross(): return lax.map(one_slot, starts_all)  19 us
    unnamed x15, local copies, waits for them, and re-layouts  13.6 us
    reduce_sum x5, other arithmetic, group_cross(): jnp.sum(left_real * right_real + left_imag * right_imag, axis=3)  4.73 us
    all_to_all x1, starting transfers between devices, on_device(): lax.all_to_all(spectra, 'seg', split_axis=3, concat_axis=1, tiled=True)  4.24 us
  transfers between devices with their start and end apart: 3, of which 3 were waited for; matrix products, arithmetic and copies ran while one was open for 2% of the time, Pallas kernels for 0%

commit v1 on v0

--- a/solution.py
+++ b/solution.py
@@ -82,7 +82,8 @@
         exact.reshape(2 * width, LAGS),
         precision=lax.Precision.HIGHEST,
     )
-    lag_sum = lax.psum(lag_terms, "seg")
+    parts = lax.all_gather(lag_terms, "seg")
+    lag_sum = jnp.sum(parts, axis=0)
     residual = (keep * jnp.tanh(scale * lag_sum - observe_flat)).astype(jnp.bfloat16)
     matrix = kernel.reshape(2 * width, LAGS)
     gamma = scale * lax.dot_general(

time: 209 us -> 196 us (0.938)
  waiting for transfers between devices: 103 us -> 90.1 us
    psum x1 -> x0, waiting for transfers between devices: 32.7 us -> none  [on_device(): lag_sum = lax.psum(lag_terms, 'seg')]
    all_gather x0 -> x1, waiting for transfers between devices: none -> 19.3 us  [on_device(): parts = lax.all_gather(lag_terms, 'seg')]
    another operation x0 -> x2, other arithmetic: none -> 2.51 us
    cos x1 -> x0, other arithmetic: 2.46 us -> none  [lag_kernel(): jnp.cos(angle)]
    unnamed x15 -> x13, local copies, waits for them, and re-layouts: 13.6 us -> 13.6 us
where the time goes in v1:
time: 196 us; the launch traced here: 195 us
  waiting for transfers between devices  90.1 us (46%)
  blocking collectives  32.9 us (17%)
  local copies, waits for them, and re-layouts  21.4 us (11%)
  loops' own time  19 us (10%)
  between operations  14.4 us (7%)
  other arithmetic  11.1 us (6%)
  starting transfers between devices  4.28 us (2%)
  matrix products  2.13 us (1%)
    unnamed x3, waiting for transfers between devices  69.1 us
    all_gather x1, blocking collectives, on_device(): gathered = lax.all_gather(local, 'sta', axis=0, tiled=True)  32.9 us
    all_gather x1, waiting for transfers between devices, on_device(): parts = lax.all_gather(lag_terms, 'seg')  19.3 us
    another operation x1, loops' own time, slot_cross(): return lax.map(one_slot, starts_all)  19 us
    unnamed x13, local copies, waits for them, and re-layouts  13.6 us
    reduce_sum x5, other arithmetic, group_cross(): jnp.sum(left_real * right_real + left_imag * right_imag, axis=3)  4.73 us
    all_to_all x1, starting transfers between devices, on_device(): lax.all_to_all(spectra, 'seg', split_axis=3, concat_axis=1, tiled=True)  4.24 us
  transfers between devices with their start and end apart: 3, of which 3 were waited for; matrix products, arithmetic and copies ran while one was open for 2% of the time, Pallas kernels for 0%

profile of v1, /device:TPU:0, one launch (start us, length us, event | category | flops | bytes accessed | tf_op | source)
XLA Modules:
  0.0 195.3 jit_solution(11775892495471226098)
XLA Ops:
  6.5 2.7 %copy.23 = bf16[6,4,2,1024]{0,1,2,3:T(4,128)(2,1)S(1)} copy(bf16[6,4,2,1024]{3,2,1,0:T(2,128)(2,1)} %param.5) | data formatting | bytes 196608 | tf_op args[0]
  9.2 4.1 %reshape.296 = bf16[4,2,6144]{2,1,0:T(2,128)(2,1)} reshape(bf16[1024,2,4,6]{3,2,1,0:T(4,128)(2,1)S(1)} %bitcast.67) | data formatting | bytes 196608
  13.3 4.2 %all-to-all-start = ((bf16[4,2,6144]{2,1,0:T(2,128)(2,1)}), bf16[4,2,6144]{2,1,0:T(2,128)(2,1)S(1)}, u32[]{:S(2)}, u32[]{:S(2)}) async-start(bf16[4,2,6144]{2,1,0:T(2,128)(2,1)} %reshape.296), calls=%async_computation | async-start | bytes 196608 | tf_op jit(solution)/shard_map/all_to_all | solution.py:73
  17.6 2.5 %cosine_convert_fusion = (bf16[1,256,512]{2,1,0:T(8,128)(2,1)S(1)}, bf16[1,256,512]{2,1,0:T(8,128)(2,1)S(1)}) fusion(s32[512]{0:T(512)S(1)} %iota_add_fusion, s32[256]{0:T(256)S(1)} %iota_add_fusion.1), kind=kLoop, calls=%fused_computation.26 | loop fusion | flops 2228224 | bytes 527360 | tf_op jit(solution)/shard_map/convert.6
  20.1 0.1 pad_maximum_fusion
  20.1 1.7 all-to-all-done
  21.9 4.7 %reshape.297 = bf16[1024,2,4,6]{3,2,1,0:T(4,128)(2,1)S(1)} reshape(bf16[4,2,6144]{2,1,0:T(2,128)(2,1)S(1)} %all-to-all-done) | data formatting | bytes 196608
  26.6 1.8 copy.24
  28.4 32.9 %all_gather.9 = bf16[48,16,2,256]{3,1,2,0:T(8,128)(2,1)S(1)} all-gather(bf16[6,16,2,256]{3,1,2,0:T(8,128)(2,1)S(1)} %all_to_all.16), channel_id=1, replica_groups=mesh['sta'=8,'seg'=4] {'sta'}, dimensions={0}, use_global_device_ids=true | all-gather | bytes 884736 | tf_op jit(solution)/shard_map/all_gather | solution.py:74
  61.4 0.1 copy.25
  61.4 28.5 %while.10 = (s32[]{:T(128)}, bf16[5,6,6,4,2,256]{5,3,2,1,4,0:T(4,128)(2,1)S(1)}, s32[5,2]{0,1:T(2,128)S(1)}, bf16[48,16,2,256]{3,1,0,2:T(8,128)(2,1)S(1)}, s32[]{:T(128)}, /*index=5*/s32[]{:T(128)}, s32[]{:T(128)}) while((s32[]{:T(128)}, bf16[5,6,6,4,2,256]{5,3,2,1,4,0:T(4,128)(2,1)S(1)}, s32[5,2]{0,1:T(2,128)S(1)}, ...), condition=%wide.region_3.4_spmd, body=%wide.region_0.3_spmd.sunk | while | flops 1499144 | bytes 2998473 | solution.py:39
  61.4 0.1 constant_dynamic-slice_fusion.3
  61.5 0.6 fusion.20
  65.9 0.1 reshape.300
  66.0 0.1 reshape.301
  66.1 0.9 add_reduce_fusion.2
  67.0 0.1 maximum_dynamic-update-slice_fusion.2
  67.1 0.1 constant_dynamic-slice_fusion.3
  67.2 0.6 fusion.20
  71.6 0.1 reshape.300
  71.7 0.1 reshape.301
  71.8 0.9 add_reduce_fusion.2
  72.7 0.1 maximum_dynamic-update-slice_fusion.2
  72.8 0.1 constant_dynamic-slice_fusion.3
  72.9 0.6 fusion.20
  77.3 0.1 reshape.300
  77.3 0.1 reshape.301
  77.5 0.9 add_reduce_fusion.2
  78.4 0.1 maximum_dynamic-update-slice_fusion.2
  78.5 0.1 constant_dynamic-slice_fusion.3
  78.6 0.6 fusion.20
  83.0 0.1 reshape.300
  83.0 0.1 reshape.301
  83.1 0.9 add_reduce_fusion.2
  84.1 0.1 maximum_dynamic-update-slice_fusion.2
  84.2 0.1 constant_dynamic-slice_fusion.3
  84.3 0.6 fusion.20
  88.7 0.1 reshape.300
  88.7 0.1 reshape.301
  88.8 0.9 add_reduce_fusion.2
  89.8 0.1 maximum_dynamic-update-slice_fusion.2
  89.9 1.0 convert_reduce_fusion
  90.9 0.3 copy.26
  91.2 0.1 pad.8
  91.3 1.2 convolution_bitcast_fusion
  92.7 0.1 and_convert_fusion
  92.7 19.3 %all-gather.4.cloned.1.call-done = f32[4,180,512]{2,1,0:T(8,128)} async-done(((f32[1,180,512]{2,1,0:T(8,128)}), f32[4,180,512]{2,1,0:T(8,128)}) %all-gather.4.cloned.1.call-update) | async-done | bytes 1474576 | tf_op jit(solution)/shard_map/all_gather | solution.py:85
  112.0 1.6 reduce_sum.73
  113.7 0.2 multiply_convert_fusion
  113.9 0.1 convert_element_type.68
  113.9 0.3 convolution_multiply_fusion
  114.3 0.2 reshape.285
  114.5 0.3 fusion.12
  114.8 0.1 fusion.3
  114.9 0.2 fusion.9
  115.1 0.1 pad_maximum_fusion.1
  115.2 0.1 reshape.286
  115.3 0.1 pad_maximum_fusion.2
  115.5 0.3 fusion.5
  115.8 0.3 convolution_add_fusion
  116.1 0.7 reshape.288
  116.8 0.6 dynamic-slice
  118.1 69.1 %all-reduce.3.cloned.1.call-done = f32[48,2,256]{2,1,0:T(2,128)} async-done(((f32[48,2,256]{2,1,0:T(2,128)}), f32[48,2,256]{2,1,0:T(2,128)}) %all-reduce.3.cloned.1.call-update) | async-done | bytes 98320
  187.2 1.3 constant_dynamic-slice_fusion.1
  (37 shorter events, 0.7 us)
Async XLA Ops:
  6.5 11.1 %copy-start.1 = (s32[5,2]{0,1:T(2,128)S(1)}, s32[5,2]{0,1:T(2,128)}, u32[]{:S(2)}) copy-start(s32[5,2]{0,1:T(2,128)} %param.7) | copy-start | bytes 124
  13.3 8.5 %all-to-all-start = ((bf16[4,2,6144]{2,1,0:T(2,128)(2,1)}), bf16[4,2,6144]{2,1,0:T(2,128)(2,1)S(1)}, u32[]{:S(2)}, u32[]{:S(2)}) async-start(bf16[4,2,6144]{2,1,0:T(2,128)(2,1)} %reshape.296), calls=%async_computation | async-start | bytes 196608 | tf_op jit(solution)/shard_map/all_to_all | solution.py:73
  17.6 94.4 %all-gather.4.cloned.1.call-start = ((), (), s32[]{:S(2)}) async-start(), calls=%async_computation.1 | async-start | bytes 1884160 | tf_op jit(solution)/shard_map/all_gather | solution.py:85
  92.5 21.1 %copy-start = (f32[5,6,6,512]{3,2,1,0:T(8,128)S(1)}, f32[5,6,6,512]{3,2,1,0:T(8,128)}, u32[]{:S(2)}) copy-start(f32[5,6,6,512]{3,2,1,0:T(8,128)} %param.6) | copy-start | bytes 1105924
  92.6 94.6 %all-reduce.3.cloned.1.call-start = ((), (), s32[]{:S(2)}) async-start(), calls=%async_computation.2 | async-start | bytes 196608
  114.5 2.3 %copy-start.2 = (u32[32]{0:T(128)S(1)}, u32[32]{0:T(128)}, u32[]{:S(2)}) copy-start(u32[32]{0:T(128)} %constant.56) | copy-start | bytes 388
Sparse Core Ops, SparseCore 0:
  92.7 19.2 all-gather.3
  117.0 70.1 all-reduce.2
